TPU v7x, 32 devices: a whole 2x2x4 slice. The times are simulated.
32 devices in a mesh: rep: 4 (over x, core), shard: 8 (over z, y).
Axes of the slice: x: 2, y: 2, z: 4, core: 2. Of those that a mesh axis runs over, the one named last changes fastest.
Arguments:
- layer_input: bfloat16 [32, 1024, 768], P(('rep', 'shard')), may hold values from -6 to 6
- in_weight: bfloat16 [768, 2304], P('shard'), may hold values from -0.21875 to 0.21875
- query_bias: bfloat16 [768], P('shard'), may hold values from -4 to 4
- value_bias: bfloat16 [768], P('shard'), may hold values from -1.5 to 1.5
- out_weight: bfloat16 [768, 768], P('shard'), may hold values from -0.875 to 0.875
- out_bias: bfloat16 [768], P('shard'), may hold values from -3 to 3
- first_gain: bfloat16 [768], P('shard'), may hold values from 0.5 to 1.5
- first_shift: bfloat16 [768], P('shard'), may hold values from -3 to 3
- inner_weight: bfloat16 [768, 3072], P('shard'), may hold values from -0.21875 to 0.21875
- inner_bias: bfloat16 [3072], P('shard'), may hold values from -4 to 4
- outer_weight: bfloat16 [3072, 768], P('shard'), may hold values from -0.15625 to 0.15625
- outer_bias: bfloat16 [768], P('shard'), may hold values from -3 to 3
- second_gain: bfloat16 [768], P('shard'), may hold values from 0.5 to 1.5
- second_shift: bfloat16 [768], P('shard'), may hold values from -3 to 3
- segment_ids: int32 [32, 1024], P(('rep', 'shard')), may hold values from 0 to 3, never falling along the last dimension, each value on 1 to 512 neighbouring positions
- token_valid: int32 [32, 1024], P(('rep', 'shard')), may hold values from 0 to 1, as said below
- query_perm: int32 [32, 12, 1024], P(('rep', 'shard')), may hold values from 0 to 1023, each once within a row
- key_perm: int32 [32, 12, 1024], P(('rep', 'shard')), may hold values from 0 to 1023, each once within a row
- out_cotangent: bfloat16 [32, 1024, 768], P(('rep', 'shard')), may hold values from -6 to 6
Outputs:
- hidden_out: bfloat16 [32, 1024, 768], P(('rep', 'shard'))
- input_grad: bfloat16 [32, 1024, 768], P(('rep', 'shard'))
- grad_in_weight: float32 [768, 2304], P('shard')
- grad_query_bias: float32 [768], P('shard')
- grad_value_bias: float32 [768], P('shard')
- grad_out_weight: float32 [768, 768], P('shard')
- grad_out_bias: float32 [768], P('shard')
- grad_first_gain: float32 [768], P('shard')
- grad_first_shift: float32 [768], P('shard')
- grad_inner_weight: float32 [768, 3072], P('shard')
- grad_inner_bias: float32 [3072], P('shard')
- grad_outer_weight: float32 [3072, 768], P('shard')
- grad_outer_bias: float32 [768], P('shard')
- grad_second_gain: float32 [768], P('shard')
- grad_second_shift: float32 [768], P('shard')
Inputs may be any that keep to these rules, and one draw needn't show every extreme that they name: `token_valid`: in each sequence the real tokens come first and at least one last position is padding (0), at most 128 positions. `segment_ids`: numbers never fall along a sequence. `query_perm`: for each sequence and head, a permutation of the positions. `key_perm`: for each sequence and head, a permutation of the positions.
All inputs are finite; a program needn't handle non-finite values.
Results may differ from a plain program's by a relative error of at most 0.015.
Values may be sent and summed in bfloat16 or wider, within the bound.
A program may use at most 256 MiB of HBM per device.

v0:
```python
from functools import partial
import jax
import jax.numpy as jnp
from jax import lax
from jax.sharding import PartitionSpec as P

CL = 128
EPS = 1e-06


def norm_parts(resid):
    average = jnp.mean(resid, axis=-1, keepdims=True)
    centred = resid - average
    variance = jnp.mean(centred * centred, axis=-1, keepdims=True)
    inv_std = lax.rsqrt(variance + EPS)
    return (centred * inv_std, inv_std)


def norm_back(grad_out, normed, inv_std, gain):
    scaled = grad_out * gain
    first_term = jnp.mean(scaled, axis=-1, keepdims=True)
    second_term = jnp.mean(scaled * normed, axis=-1, keepdims=True)
    grad_in = inv_std * (scaled - first_term - normed * second_term)
    return (grad_in, jnp.sum(grad_out * normed, axis=0), jnp.sum(grad_out, axis=0))


def invert_order(order):

    def single(row_order):
        return (
            jnp.zeros_like(row_order)
            .at[row_order]
            .set(jnp.arange(row_order.shape[0], dtype=jnp.int32))
        )

    return jax.vmap(jax.vmap(single))(order)


def to_heads(tensor, seqs, heads):
    tokens, width = tensor.shape
    return jnp.transpose(tensor.reshape(seqs, tokens // seqs, heads, width // heads), (0, 2, 1, 3))


def from_heads(tensor):
    seqs, heads, length, head_size = tensor.shape
    return jnp.transpose(tensor, (0, 2, 1, 3)).reshape(seqs * length, heads * head_size)


def arrange(tensor, order):
    return jnp.take_along_axis(tensor, order[..., None], axis=2)


def in_clusters(tensor):
    seqs, heads, length, inner_dim = tensor.shape
    return tensor.reshape(seqs, heads, length // CL, CL, inner_dim)


def shards(
    layer_input,
    in_weight,
    query_bias,
    value_bias,
    out_weight,
    out_bias,
    first_gain,
    first_shift,
    inner_weight,
    inner_bias,
    outer_weight,
    outer_bias,
    second_gain,
    second_shift,
    segment_ids,
    token_valid,
    query_perm,
    key_perm,
    out_cotangent,
):
    seqs, length, width = layer_input.shape
    heads = query_perm.shape[1]
    head_size = width // heads
    scale = head_size ** (-0.5)
    tokens = seqs * length
    gathered = (
        lax.all_gather(in_weight, "shard", axis=0, tiled=True),
        lax.all_gather(query_bias, "shard", axis=0, tiled=True),
        lax.all_gather(value_bias, "shard", axis=0, tiled=True),
        lax.all_gather(out_weight, "shard", axis=0, tiled=True),
        lax.all_gather(out_bias, "shard", axis=0, tiled=True),
        lax.all_gather(first_gain, "shard", axis=0, tiled=True),
        lax.all_gather(first_shift, "shard", axis=0, tiled=True),
        lax.all_gather(inner_weight, "shard", axis=0, tiled=True),
        lax.all_gather(inner_bias, "shard", axis=0, tiled=True),
        lax.all_gather(outer_weight, "shard", axis=0, tiled=True),
        lax.all_gather(outer_bias, "shard", axis=0, tiled=True),
        lax.all_gather(second_gain, "shard", axis=0, tiled=True),
        lax.all_gather(second_shift, "shard", axis=0, tiled=True),
    )
    (
        w_in,
        b_query,
        b_value,
        w_out,
        b_out,
        g_first,
        s_first,
        w_inner,
        b_inner,
        w_outer,
        b_outer,
        g_second,
        s_second,
    ) = gathered
    flat_in = layer_input.reshape(tokens, width)
    projected = jnp.dot(flat_in, w_in, preferred_element_type=jnp.float32)
    query = (projected[:, :width] + b_query.astype(jnp.float32)).astype(jnp.bfloat16)
    keys = projected[:, width : 2 * width].astype(jnp.bfloat16)
    values = (projected[:, 2 * width :] + b_value.astype(jnp.float32)).astype(jnp.bfloat16)
    q_cl = in_clusters(arrange(to_heads(query, seqs, heads), query_perm))
    k_cl = in_clusters(arrange(to_heads(keys, seqs, heads), key_perm))
    v_cl = in_clusters(arrange(to_heads(values, seqs, heads), key_perm))
    seg_heads = jnp.broadcast_to(segment_ids[:, None, :], query_perm.shape)
    ok_heads = jnp.broadcast_to(token_valid[:, None, :], query_perm.shape)
    cshape = (seqs, heads, length // CL, CL)
    seg_query = jnp.take_along_axis(seg_heads, query_perm, axis=2).reshape(cshape)
    seg_key = jnp.take_along_axis(seg_heads, key_perm, axis=2).reshape(cshape)
    ok_query = jnp.take_along_axis(ok_heads, query_perm, axis=2).reshape(cshape)
    ok_key = jnp.take_along_axis(ok_heads, key_perm, axis=2).reshape(cshape)
    visible = (
        (seg_query[..., :, None] == seg_key[..., None, :])
        & (ok_query[..., :, None] > 0)
        & (ok_key[..., None, :] > 0)
    )
    scores = (
        jnp.einsum("shcie,shcje->shcij", q_cl, k_cl, preferred_element_type=jnp.float32) * scale
    )
    maxima = jnp.max(jnp.where(visible, scores, -1e30), axis=-1, keepdims=True)
    raised = jnp.where(visible, jnp.exp(jnp.where(visible, scores - maxima, 0.0)), 0.0)
    divisor = jnp.maximum(jnp.sum(raised, axis=-1, keepdims=True), 1.0)
    probs_low = (raised / divisor).astype(jnp.bfloat16)
    log_total = maxima + jnp.log(divisor)
    combined = jnp.einsum("shcij,shcje->shcie", probs_low, v_cl, preferred_element_type=jnp.float32)
    query_back = invert_order(query_perm)
    key_back = invert_order(key_perm)
    attended = from_heads(
        arrange(combined.reshape(seqs, heads, length, head_size), query_back)
    ).astype(jnp.bfloat16)
    branch = jnp.dot(attended, w_out, preferred_element_type=jnp.float32) + b_out.astype(
        jnp.float32
    )
    first_sum = flat_in.astype(jnp.float32) + branch
    normed_first, inv_first = norm_parts(first_sum)
    first_out = normed_first * g_first.astype(jnp.float32) + s_first.astype(jnp.float32)
    first_low = first_out.astype(jnp.bfloat16)
    inner = jnp.dot(first_low, w_inner, preferred_element_type=jnp.float32) + b_inner.astype(
        jnp.float32
    )
    activated = jax.nn.gelu(inner, approximate=False).astype(jnp.bfloat16)
    outer = jnp.dot(activated, w_outer, preferred_element_type=jnp.float32) + b_outer.astype(
        jnp.float32
    )
    normed_second, inv_second = norm_parts(first_out + outer)
    hidden_out = (
        (normed_second * g_second.astype(jnp.float32) + s_second.astype(jnp.float32))
        .astype(jnp.bfloat16)
        .reshape(seqs, length, width)
    )
    back_in, back_out, back_inner, back_outer, back_gfirst, back_gsecond = (
        w_in,
        w_out,
        w_inner,
        w_outer,
        g_first,
        g_second,
    )
    grad_top = out_cotangent.reshape(tokens, width).astype(jnp.float32)
    d_second, grad_g_second, grad_s_second = norm_back(
        grad_top, normed_second, inv_second, back_gsecond.astype(jnp.float32)
    )
    d_outer = d_second.astype(jnp.bfloat16)
    grad_b_outer = jnp.sum(d_outer, axis=0, dtype=jnp.float32)
    d_activated = jnp.einsum("td,fd->tf", d_outer, back_outer, preferred_element_type=jnp.float32)
    unused, gelu_pull = jax.vjp(partial(jax.nn.gelu, approximate=False), inner)
    d_inner = gelu_pull(d_activated)[0].astype(jnp.bfloat16)
    grad_b_inner = jnp.sum(d_inner, axis=0, dtype=jnp.float32)
    d_first_out = d_second + jnp.einsum(
        "tf,df->td", d_inner, back_inner, preferred_element_type=jnp.float32
    )
    d_first, grad_g_first, grad_s_first = norm_back(
        d_first_out, normed_first, inv_first, back_gfirst.astype(jnp.float32)
    )
    d_branch = d_first.astype(jnp.bfloat16)
    grad_b_out = jnp.sum(d_branch, axis=0, dtype=jnp.float32)
    d_attended = jnp.einsum(
        "te,de->td", d_branch, back_out, preferred_element_type=jnp.float32
    ).astype(jnp.bfloat16)
    do_cl = in_clusters(arrange(to_heads(d_attended, seqs, heads), query_perm))
    again_scores = (
        jnp.einsum("shcie,shcje->shcij", q_cl, k_cl, preferred_element_type=jnp.float32) * scale
    )
    probs = jnp.where(visible, jnp.exp(jnp.where(visible, again_scores - log_total, 0.0)), 0.0)
    d_probs = jnp.einsum("shcie,shcje->shcij", do_cl, v_cl, preferred_element_type=jnp.float32)
    row_terms = jnp.sum(probs * d_probs, axis=-1, keepdims=True)
    d_scores = (probs * (d_probs - row_terms)).astype(jnp.bfloat16)
    dq_cl = (
        jnp.einsum("shcij,shcje->shcie", d_scores, k_cl, preferred_element_type=jnp.float32) * scale
    )
    dk_cl = (
        jnp.einsum("shcij,shcie->shcje", d_scores, q_cl, preferred_element_type=jnp.float32) * scale
    )
    dv_cl = jnp.einsum(
        "shcij,shcie->shcje", probs.astype(jnp.bfloat16), do_cl, preferred_element_type=jnp.float32
    )

    def restore(clustered, back_order):
        return from_heads(arrange(clustered.reshape(seqs, heads, length, head_size), back_order))

    d_proj = jnp.concatenate(
        [restore(dq_cl, query_back), restore(dk_cl, key_back), restore(dv_cl, key_back)], axis=1
    ).astype(jnp.bfloat16)
    grad_b_query = jnp.sum(d_proj[:, :width], axis=0, dtype=jnp.float32)
    grad_b_value = jnp.sum(d_proj[:, 2 * width :], axis=0, dtype=jnp.float32)
    input_grad = (
        (d_first + jnp.einsum("te,de->td", d_proj, back_in, preferred_element_type=jnp.float32))
        .astype(jnp.bfloat16)
        .reshape(seqs, length, width)
    )
    local_shapes = [
        in_weight.shape,
        query_bias.shape,
        value_bias.shape,
        out_weight.shape,
        out_bias.shape,
        first_gain.shape,
        first_shift.shape,
        inner_weight.shape,
        inner_bias.shape,
        outer_weight.shape,
        outer_bias.shape,
        second_gain.shape,
        second_shift.shape,
    ]

    def product_rows(left, right):
        return jnp.einsum("tk,te->ke", left, right, preferred_element_type=jnp.float32).reshape(
            lax.axis_size("shard") * 1, -1
        )

    def vector_rows(vector):
        return vector.reshape(lax.axis_size("shard") * 1, -1)

    pieces = [
        product_rows(flat_in, d_proj),
        vector_rows(grad_b_query),
        vector_rows(grad_b_value),
        product_rows(attended, d_branch),
        vector_rows(grad_b_out),
        vector_rows(grad_g_first),
        vector_rows(grad_s_first),
        product_rows(first_low, d_inner),
        vector_rows(grad_b_inner),
        product_rows(activated, d_outer),
        vector_rows(grad_b_outer),
        vector_rows(grad_g_second),
        vector_rows(grad_s_second),
    ]
    my_rows = lax.psum_scatter(
        jnp.concatenate(pieces, axis=1), "shard", scatter_dimension=0, tiled=True
    )
    my_rows = lax.psum(my_rows.astype(jnp.bfloat16), "rep").astype(jnp.float32)
    flat_mine = my_rows.reshape(-1)
    results = []
    offset = 0
    for shape_here in local_shapes:
        count_here = 1
        for extent_here in shape_here:
            count_here = count_here * extent_here
        results.append(flat_mine[offset : offset + count_here].reshape(shape_here))
        offset = offset + count_here
    return (
        hidden_out,
        input_grad,
        results[0],
        results[1],
        results[2],
        results[3],
        results[4],
        results[5],
        results[6],
        results[7],
        results[8],
        results[9],
        results[10],
        results[11],
        results[12],
    )


def solution(mesh):
    return jax.shard_map(
        shards,
        mesh=mesh,
        in_specs=(
            P(("rep", "shard"), None, None),
            P("shard", None),
            P("shard"),
            P("shard"),
            P("shard", None),
            P("shard"),
            P("shard"),
            P("shard"),
            P("shard", None),
            P("shard"),
            P("shard", None),
            P("shard"),
            P("shard"),
            P("shard"),
            P(("rep", "shard"), None),
            P(("rep", "shard"), None),
            P(("rep", "shard"), None, None),
            P(("rep", "shard"), None, None),
            P(("rep", "shard"), None, None),
        ),
        out_specs=(
            P(("rep", "shard"), None, None),
            P(("rep", "shard"), None, None),
            P("shard", None),
            P("shard"),
            P("shard"),
            P("shard", None),
            P("shard"),
            P("shard"),
            P("shard"),
            P("shard", None),
            P("shard"),
            P("shard", None),
            P("shard"),
            P("shard"),
            P("shard"),
        ),
        check_vma=False,
    )
```

profile of v0, /device:TPU:0, one launch (start us, length us, event | category | flops | bytes accessed | tf_op | source)
XLA Modules:
  0.0 3090.1 jit_solution(8853044434371541928)
XLA Ops:
  13.8 97.2 %gather_fusion.2 = s32[12288]{0:T(1024)S(1)} fusion(s32[12,1024]{1,0:T(8,128)S(1)} %broadcast.664, s32[12288]{0:T(1024)S(1)} %bitcast.233), kind=kCustom, calls=%fused_computation.4.clone | custom fusion | bytes 196608 | tf_op jit(solution)/shard_map/jit(take_along_axis)/gather | solution.py:127
  111.1 97.2 %gather_fusion = s32[12288]{0:T(1024)S(1)} fusion(s32[12,1024]{1,0:T(8,128)S(1)} %broadcast.662, s32[12288]{0:T(1024)S(1)} %bitcast.234), kind=kCustom, calls=%fused_computation.clone | custom fusion | bytes 196608 | tf_op jit(solution)/shard_map/jit(take_along_axis)/gather | solution.py:125
  208.4 97.2 %gather_fusion.3 = s32[12288]{0:T(1024)S(1)} fusion(s32[12,1024]{1,0:T(8,128)S(1)} %broadcast.664, s32[12288]{0:T(1024)S(1)} %bitcast.235), kind=kCustom, calls=%fused_computation.5.clone | custom fusion | bytes 196608 | tf_op jit(solution)/shard_map/jit(take_along_axis)/gather | solution.py:128
  305.8 97.2 %gather_fusion.1 = s32[12288]{0:T(1024)S(1)} fusion(s32[12,1024]{1,0:T(8,128)S(1)} %broadcast.662, s32[12288]{0:T(1024)S(1)} %bitcast.236), kind=kCustom, calls=%fused_computation.3.clone | custom fusion | bytes 196608 | tf_op jit(solution)/shard_map/jit(take_along_axis)/gather | solution.py:126
  404.7 45.4 %scatter_custom_fusion.1 = s32[12288]{0:T(1024)S(1)} fusion(s32[12288]{0:T(1024)S(1)} %reshape.572, s32[12288]{0:T(1024)S(1)} %reshape.566, s32[]{:T(128)} %constant.12.clone.1), kind=kCustom, calls=%fused_computation.151 | custom fusion | bytes 49156
  450.9 45.4 %scatter_custom_fusion = s32[12288]{0:T(1024)S(1)} fusion(s32[12288]{0:T(1024)S(1)} %reshape.564, s32[12288]{0:T(1024)S(1)} %reshape.566, s32[]{:T(128)} %constant.12.clone.1), kind=kCustom, calls=%fused_computation.153 | custom fusion | bytes 49156
  499.6 38.8 %all-reduce.9 = (bf16[768]{0:T(1024)(128)(2,1)S(1)}, bf16[768]{0:T(1024)(128)(2,1)S(1)}, bf16[768]{0:T(1024)(128)(2,1)S(1)}, bf16[768]{0:T(1024)(128)(2,1)S(1)},...) all-reduce(bf16[768]{0:T(1024)(128)(2,1)S(1)} %dynamic-update-slice, ...), channel_id=1, replica_groups=mesh['rep'=4,'shard'=8] {'shard'}, use_global_device_ids=true, to_apply=%add | all-reduce | flops 6144 | bytes 24576
  540.2 25.9 all-gather
  572.3 5.8 fusion.27
  583.3 3.1 copy.97
  586.3 119.4 %gather_fusion.5 = bf16[12288,64]{1,0:T(8,128)(2,1)} fusion(bf16[12,1024,64]{2,1,0:T(8,128)(2,1)S(1)} %bitcast.237, s32[12288]{0:T(1024)S(1)} %bitcast.231), kind=kCustom, calls=%fused_computation.6.clone | custom fusion | bytes 3244032 | tf_op jit(solution)/shard_map/jit(take_along_axis)/gather | solution.py:50
  705.7 4.3 copy.98
  710.0 3.1 copy.102
  713.0 119.4 %gather_fusion.6 = bf16[12288,64]{1,0:T(8,128)(2,1)} fusion(bf16[12,1024,64]{2,1,0:T(8,128)(2,1)S(1)} %bitcast.238, s32[12288]{0:T(1024)S(1)} %bitcast.232), kind=kCustom, calls=%fused_computation.7.clone | custom fusion | bytes 3244032 | tf_op jit(solution)/shard_map/jit(take_along_axis)/gather | solution.py:50
  832.4 3.2 copy.103
  840.9 3.1 copy.94
  844.0 119.4 %gather_fusion.4 = bf16[12288,64]{1,0:T(8,128)(2,1)} fusion(bf16[12,1024,64]{2,1,0:T(8,128)(2,1)S(1)} %bitcast.239, s32[12288]{0:T(1024)S(1)} %bitcast.229), kind=kCustom, calls=%fused_computation.1.clone | custom fusion | bytes 3244032 | tf_op jit(solution)/shard_map/jit(take_along_axis)/gather | solution.py:50
  963.3 3.2 copy.95
  967.2 12.3 select_reduce_fusion
  979.6 4.9 fusion.11
  985.1 8.2 fusion.20
  993.4 119.5 %gather_fusion.7 = bf16[12288,64]{1,0:T(8,128)(2,1)} fusion(bf16[12,1024,64]{2,1,0:T(8,128)(2,1)S(1)} %bitcast.244, s32[12288]{0:T(1024)S(1)} %reshape.741), kind=kCustom, calls=%fused_computation.2.clone | custom fusion | bytes 3244032 | tf_op jit(solution)/shard_map/jit(take_along_axis)/gather | solution.py:50
  1112.9 3.1 copy.108
  1117.6 3.9 fusion.63
  1122.0 38.7 %multiply_convert_fusion = (bf16[1024,3072]{1,0:T(8,128)(2,1)}, f32[1024,3072]{1,0:T(8,128)}, f32[1024,3072]{1,0:T(8,128)}) fusion(f32[3072]{0:T(1024)S(1)} %bitcast.302, bf16[768,3072]{1,0:T(8,128)(2,1)} %all-gather.10.cloned.1.call-done, f32[1024,768]{0,1:T(8,128)S(1)} %get-tuple-element.122, f32[768]{0:T(1024)S(1)} %convert_element_type.123, ...), kind=kOutput, calls=%fused_computation.18 | convolution fusion | flops 5043388416 | bytes 39348224 | tf_op jit(solution)/shard_map/dot_general | solution.py:155
  1160.7 9.8 fusion.64
  1174.9 7.5 fusion.65
  1182.4 17.4 convert_reduce_fusion
  1199.9 10.6 fusion.56
  1210.5 9.0 multiply_reduce_fusion.1
  1220.9 2.8 fusion.47
  1226.3 3.1 copy.112
  1229.4 119.4 %gather_fusion.8 = bf16[12288,64]{1,0:T(8,128)(2,1)} fusion(bf16[12,1024,64]{2,1,0:T(8,128)(2,1)S(1)} %bitcast.240, s32[12288]{0:T(1024)S(1)} %bitcast.230), kind=kCustom, calls=%fused_computation.8.clone | custom fusion | bytes 3244032 | tf_op jit(solution)/shard_map/jit(take_along_axis)/gather | solution.py:50
  1348.8 3.2 copy.113
  1352.7 8.2 fusion.18
  1360.9 12.2 multiply_reduce_fusion
  1373.1 5.0 multiply_convert_fusion.1
  1378.2 3.4 convolution_multiply_fusion.1
  1384.1 9.0 reshape.425
  1393.2 3.5 reshape.421
  1399.2 120.2 %gather_fusion.11 = bf16[12288,64]{1,0:T(8,128)(2,1)} fusion(bf16[12,1024,64]{2,1,0:T(8,128)(2,1)S(1)} %bitcast.243, s32[12288]{0:T(1024)S(1)} %copy-done.4), kind=kCustom, calls=%fused_computation.11.clone | custom fusion | bytes 3244032 | tf_op jit(solution)/shard_map/jit(take_along_axis)/gather | solution.py:50
  1519.4 4.5 copy.130
  1523.9 9.0 reshape.427
  1532.9 3.1 copy.143
  1536.0 120.3 %gather_fusion.9 = bf16[12288,64]{1,0:T(8,128)(2,1)} fusion(bf16[12,1024,64]{2,1,0:T(8,128)(2,1)S(1)} %bitcast.241, s32[12288]{0:T(1024)S(1)} %copy-done.6), kind=kCustom, calls=%fused_computation.9.clone | custom fusion | bytes 3244032 | tf_op jit(solution)/shard_map/jit(take_along_axis)/gather | solution.py:50
  1656.3 3.1 copy.120
  1661.4 3.1 copy.144
  1664.5 120.3 %gather_fusion.10 = bf16[12288,64]{1,0:T(8,128)(2,1)} fusion(bf16[12,1024,64]{2,1,0:T(8,128)(2,1)S(1)} %bitcast.242, s32[12288]{0:T(1024)S(1)} %copy-done.4), kind=kCustom, calls=%fused_computation.10.clone | custom fusion | bytes 3244032 | tf_op jit(solution)/shard_map/jit(take_along_axis)/gather | solution.py:50
  1784.8 4.3 copy.125
  1789.1 4.2 select_convert_fusion.1
  1793.7 8.9 convolution_bitcast_fusion
  1802.6 8.0 copy.132
  1810.6 7.2 reshape.418
  1817.8 5.3 constant_dynamic-update-slice_fusion
  1826.2 7.5 dynamic-update-slice.11
  1837.9 26.4 dynamic-update-slice.15
  1865.8 26.0 dynamic-update-slice.17
  1896.0 1069.1 %all-reduce.14 = bf16[8,885888]{1,0:T(8,128)(2,1)} all-reduce(f32[8,885888]{1,0:T(8,128)} %dynamic-update-slice.20), channel_id=2, replica_groups=mesh['rep'=4,'shard'=8] {'shard'}, use_global_device_ids=true, to_apply=%region_22.26.clone | all-reduce | flops 7087104 | bytes 42522624
  2965.1 9.1 dynamic-slice_convert_fusion
  2974.2 8.5 fusion.29
  2985.3 63.7 %all-reduce.13.cloned.1.call-done = bf16[1,885888]{1,0:T(2,128)(2,1)} async-done(((bf16[1,885888]{1,0:T(2,128)(2,1)}), bf16[1,885888]{1,0:T(2,128)(2,1)}) %all-reduce.13.cloned.1.call-update) | async-done | bytes 1771792 | tf_op jit(solution)/shard_map/psum | solution.py:270
  3049.0 6.3 convert_element_type.146
  3057.3 9.1 slice_reduce_fusion.2
  3066.5 12.7 slice_reduce_fusion
  (276 shorter events, 71.2 us)
Async XLA Ops:
  7.2 6.6 copy-start
  7.2 565.1 %all-gather.6.cloned.1.call-start = ((), (), s32[]{:S(2)}) async-start(), calls=%async_computation | async-start | bytes 3981312 | tf_op jit(solution)/shard_map/all_gather | solution.py:85
  7.9 1109.7 %all-gather.8.cloned.1.call-start = ((), (), s32[]{:S(2)}) async-start(), calls=%async_computation.1 | async-start | bytes 1327104 | tf_op jit(solution)/shard_map/all_gather | solution.py:88
  8.7 1113.3 %all-gather.10.cloned.1.call-start = ((), (), s32[]{:S(2)}) async-start(), calls=%async_computation.2 | async-start | bytes 5308416 | tf_op jit(solution)/shard_map/all_gather | solution.py:92
  9.4 1151.3 %all-gather.12.cloned.1.call-start = ((), (), s32[]{:S(2)}) async-start(), calls=%async_computation.3 | async-start | bytes 5308416 | tf_op jit(solution)/shard_map/all_gather | solution.py:94
  10.0 3039.0 %all-reduce.13.cloned.1.call-start = ((), (), s32[]{:S(2)}) async-start(), calls=%async_computation.4 | async-start | bytes 7087104 | tf_op jit(solution)/shard_map/psum | solution.py:270
  11.9 832.0 %copy-start.2 = (s32[12,1024,1]{1,2,0:T(1,128)}, s32[12,1024,1]{1,2,0:T(1,128)S(1)}, u32[]{:S(2)}) copy-start(s32[12,1024,1]{1,2,0:T(1,128)S(1)} %get-tuple-element.110) | copy-start | bytes 147460
  13.8 97.3 %copy-start.49 = (s32[1,1024]{1,0:T(1,128)S(1)}, s32[1,1024]{1,0:T(1,128)}, u32[]{:S(2)}) copy-start(s32[1,1024]{1,0:T(1,128)} %param.39) | copy-start | bytes 12292
  305.6 97.5 %copy-start.30 = (s32[1,12,1024]{2,0,1:T(1,128)S(1)}, s32[1,12,1024]{2,0,1:T(1,128)}, u32[]{:S(2)}) copy-start(s32[1,12,1024]{2,0,1:T(1,128)} %param.41) | copy-start | bytes 147460
  305.6 97.6 %copy-start.31 = (s32[1,12,1024]{2,0,1:T(1,128)S(1)}, s32[1,12,1024]{2,0,1:T(1,128)}, u32[]{:S(2)}) copy-start(s32[1,12,1024]{2,0,1:T(1,128)} %param.42) | copy-start | bytes 147460
  305.6 97.8 %copy-start.54 = (s32[3]{0:T(128)S(1)}, s32[3]{0:T(128)}, u32[]{:S(2)}) copy-start(s32[3]{0:T(128)} %constant.125) | copy-start | bytes 40
  305.6 98.4 %copy-start.53 = (s32[3]{0:T(128)S(1)}, s32[3]{0:T(128)}, u32[]{:S(2)}) copy-start(s32[3]{0:T(128)} %constant.128) | copy-start | bytes 40
  305.6 190.7 %copy-start.52 = (bf16[384]{0:T(512)(128)(2,1)S(1)}, bf16[384]{0:T(512)(128)(2,1)}, u32[]{:S(2)}) copy-start(bf16[384]{0:T(512)(128)(2,1)} %param.34) | copy-start | bytes 2308
  305.7 190.8 %copy-start.51 = (u32[32]{0:T(128)S(1)}, u32[32]{0:T(128)}, u32[]{:S(2)}) copy-start(u32[32]{0:T(128)} %constant.300) | copy-start | bytes 388
  305.7 192.0 %copy-start.56 = (bf16[96]{0:T(256)(128)(2,1)S(1)}, bf16[96]{0:T(256)(128)(2,1)}, u32[]{:S(2)}) copy-start(bf16[96]{0:T(256)(128)(2,1)} %param.38) | copy-start | bytes 580
  305.7 192.2 %copy-start.57 = (bf16[96]{0:T(256)(128)(2,1)S(1)}, bf16[96]{0:T(256)(128)(2,1)}, u32[]{:S(2)}) copy-start(bf16[96]{0:T(256)(128)(2,1)} %param.36) | copy-start | bytes 580
  305.7 192.5 %copy-start.58 = (bf16[96]{0:T(256)(128)(2,1)S(1)}, bf16[96]{0:T(256)(128)(2,1)}, u32[]{:S(2)}) copy-start(bf16[96]{0:T(256)(128)(2,1)} %param.31) | copy-start | bytes 580
  305.7 192.7 %copy-start.59 = (bf16[96]{0:T(256)(128)(2,1)S(1)}, bf16[96]{0:T(256)(128)(2,1)}, u32[]{:S(2)}) copy-start(bf16[96]{0:T(256)(128)(2,1)} %param.32) | copy-start | bytes 580
  305.7 192.9 %copy-start.60 = (bf16[96]{0:T(256)(128)(2,1)S(1)}, bf16[96]{0:T(256)(128)(2,1)}, u32[]{:S(2)}) copy-start(bf16[96]{0:T(256)(128)(2,1)} %param.30) | copy-start | bytes 580
  305.7 193.1 %copy-start.61 = (bf16[96]{0:T(256)(128)(2,1)S(1)}, bf16[96]{0:T(256)(128)(2,1)}, u32[]{:S(2)}) copy-start(bf16[96]{0:T(256)(128)(2,1)} %param.28) | copy-start | bytes 580
  305.7 193.4 %copy-start.62 = (bf16[96]{0:T(256)(128)(2,1)S(1)}, bf16[96]{0:T(256)(128)(2,1)}, u32[]{:S(2)}) copy-start(bf16[96]{0:T(256)(128)(2,1)} %param.27) | copy-start | bytes 580
  305.8 193.6 %copy-start.63 = (bf16[96]{0:T(256)(128)(2,1)S(1)}, bf16[96]{0:T(256)(128)(2,1)}, u32[]{:S(2)}) copy-start(bf16[96]{0:T(256)(128)(2,1)} %param.37) | copy-start | bytes 580
  403.0 164.4 %copy-start.25 = (bf16[1,1024,768]{2,1,0:T(8,128)(2,1)S(1)}, bf16[1,1024,768]{2,1,0:T(8,128)(2,1)}, u32[]{:S(2)}) copy-start(bf16[1,1024,768]{2,1,0:T(8,128)(2,1)} %param.43) | copy-start | bytes 4718596
  403.2 581.9 %copy-start.32 = (s32[1,12,1024]{2,0,1:T(1,128)}, s32[1,12,1024]{2,0,1:T(1,128)S(1)}, u32[]{:S(2)}) copy-start(s32[1,12,1024]{2,0,1:T(1,128)S(1)} %get-tuple-element.108) | copy-start | bytes 147460
  403.4 581.7 %copy-start.34 = (s32[1,12,1024]{2,0,1:T(1,128)}, s32[1,12,1024]{2,0,1:T(1,128)S(1)}, u32[]{:S(2)}) copy-start(s32[1,12,1024]{2,0,1:T(1,128)S(1)} %get-tuple-element.106) | copy-start | bytes 147460
  496.3 619.7 %copy-start.37 = (pred[12,1024]{1,0:T(8,128)(4,1)}, pred[12,1024]{1,0:T(8,128)(4,1)S(1)}, u32[]{:S(2)}) copy-start(pred[12,1024]{1,0:T(8,128)(4,1)S(1)} %and_bitcast_fusion.1) | copy-start | bytes 36868
  566.1 400.4 %copy-start.39 = (pred[1,12,1024,1]{2,1,3,0:T(8,128)(4,1)}, pred[1,12,1024,1]{2,1,3,0:T(8,128)(4,1)S(1)}, u32[]{:S(2)}) copy-start(pred[1,12,1024,1]{2,1,3,0:T(8,128)(4,1)S(1)} %copy.184) | copy-start | bytes 36868
  566.4 418.6 %copy-start.41 = (pred[12,8,128]{2,1,0:T(8,128)(4,1)}, pred[12,8,128]{2,1,0:T(8,128)(4,1)S(1)}, u32[]{:S(2)}) copy-start(pred[12,8,128]{2,1,0:T(8,128)(4,1)S(1)} %slice.147) | copy-start | bytes 36868
  566.7 418.4 %copy-start.43 = (pred[12,8,128]{2,1,0:T(8,128)(4,1)}, pred[12,8,128]{2,1,0:T(8,128)(4,1)S(1)}, u32[]{:S(2)}) copy-start(pred[12,8,128]{2,1,0:T(8,128)(4,1)S(1)} %slice.148) | copy-start | bytes 36868
  567.4 426.0 %copy-start.5 = (s32[12288]{0:T(1024)}, s32[12288]{0:T(1024)S(1)}, u32[]{:S(2)}) copy-start(s32[12288]{0:T(1024)S(1)} %reshape.741) | copy-start | bytes 147460
  568.6 9.5 copy-start.8
  568.6 3.6 copy-start.26
  832.4 3.2 copy-start.22
  836.0 3.3 copy-start.23
  963.3 3.9 copy-start.16
  967.2 12.3 copy-start.18
  979.5 13.8 copy-start.7
  979.6 5.5 copy-start.27
  1121.5 39.1 %copy-start.10 = (f32[1024,768]{0,1:T(8,128)}, f32[1024,768]{0,1:T(8,128)S(1)}, u32[]{:S(2)}) copy-start(f32[1024,768]{0,1:T(8,128)S(1)} %get-tuple-element.122) | copy-start | bytes 9437188
  1122.0 38.7 %copy-start.50 = (f32[768]{0:T(1024)S(1)}, f32[768]{0:T(1024)}, u32[]{:S(2)}) copy-start(f32[768]{0:T(1024)} %convert_element_type.127) | copy-start | bytes 9220
  1160.7 10.2 copy-start.9
  1160.7 10.2 copy-start.46
  1170.9 4.0 slice-start.2
  1199.8 10.6 copy-start.11
  1199.8 10.6 copy-start.64
  1348.8 3.9 copy-start.33
  1348.8 3.9 copy-start.35
  1348.8 3.9 copy-start.36
  1348.8 3.9 copy-start.42
  1348.8 3.9 copy-start.44
  1352.0 8.9 slice-start
  1352.7 8.2 slice-start.1
  1352.7 8.2 copy-start.28
  1373.1 5.1 copy-start.19
  1378.2 3.4 copy-start.17
  1393.1 6.1 copy-start.4
  1784.8 4.3 copy-start.45
  1789.1 4.6 copy-start.14
  1793.3 9.3 copy-start.20
  1817.8 8.4 copy-start.12
  1865.7 28.9 copy-start.48
  2965.1 9.1 copy-start.15
  2965.1 9.2 copy-start.21
  3066.5 17.0 copy-start.1
  (10 other events, 25.5 us)
Sparse Core Ops, SparseCore 0:
  10.2 67.8 all-gather.5
  80.3 39.5 all-gather.7
  122.1 78.6 all-gather.9
  202.8 78.0 all-gather.11
  2974.3 74.5 all-reduce.12
where the time goes:
time: 3100 us; the launch traced here: 3090 us
  local copies, waits for them, and re-layouts  1660 us (54%)
  blocking collectives  1130 us (36%)
  matrix products  172 us (6%)
  waiting for transfers between devices  66.3 us (2%)
  other arithmetic  40.3 us (1%)
    unnamed x2, blocking collectives  1110 us
    gather x18, local copies, waits for them, and re-layouts, arrange(): return jnp.take_along_axis(tensor, order[..., None], axis=2)  987 us
    unnamed x186, local copies, waits for them, and re-layouts  185 us
    gather x1, local copies, waits for them, and re-layouts, shards(): ok_query = jnp.take_along_axis(ok_heads, query_perm, axis=2).reshape(cshape)  97.2 us
    gather x1, local copies, waits for them, and re-layouts, shards(): jnp.take_along_axis(seg_heads, query_perm, axis=2).reshape(cshape)  97.2 us
    gather x1, local copies, waits for them, and re-layouts, shards(): ok_key = jnp.take_along_axis(ok_heads, key_perm, axis=2).reshape(cshape)  97.2 us
    gather x1, local copies, waits for them, and re-layouts, shards(): seg_key = jnp.take_along_axis(seg_heads, key_perm, axis=2).reshape(cshape)  97.2 us
    psum x1, waiting for transfers between devices, shards(): my_rows = lax.psum(my_rows.astype(jnp.bfloat16), 'rep').astype(jnp.float32)  63.7 us
  transfers between devices with their start and end apart: 5, of which 1 were waited for; matrix products, arithmetic and copies ran while one was open for 35% of the time, Pallas kernels for 0%

commit v1 on v0

--- a/solution.py
+++ b/solution.py
@@ -6,6 +6,11 @@
 
 CL = 128
 EPS = 1e-06
+
+
+def add_all(array, mesh_axis):
+    pieces = lax.all_gather(array, mesh_axis)
+    return jnp.sum(pieces, axis=0)
 
 
 def norm_parts(resid):
@@ -267,7 +272,7 @@
     my_rows = lax.psum_scatter(
         jnp.concatenate(pieces, axis=1), "shard", scatter_dimension=0, tiled=True
     )
-    my_rows = lax.psum(my_rows.astype(jnp.bfloat16), "rep").astype(jnp.float32)
+    my_rows = add_all(my_rows.astype(jnp.bfloat16), "rep").astype(jnp.float32)
     flat_mine = my_rows.reshape(-1)
     results = []
     offset = 0

time: 3100 us -> 3170 us (1.023)
  other arithmetic: 40.3 us -> 72.3 us
    all_gather x0 -> x1, waiting for transfers between devices: none -> 79.8 us  [add_all(): pieces = lax.all_gather(array, mesh_axis)]
    psum x1 -> x0, waiting for transfers between devices: 63.7 us -> none  [shards(): my_rows = lax.psum(my_rows.astype(jnp.bfloat16), 'rep').astype(jnp.float32)]
    reduce_sum x0 -> x1, other arithmetic: none -> 38.3 us  [add_all(): return jnp.sum(pieces, axis=0)]
    unnamed x186 -> x187, local copies, waits for them, and re-layouts: 185 us -> 192 us
where the time goes in v1:
time: 3170 us; the launch traced here: 3160 us
  local copies, waits for them, and re-layouts  1680 us (53%)
  blocking collectives  1130 us (36%)
  matrix products  171 us (5%)
  waiting for transfers between devices  82.4 us (3%)
  other arithmetic  72.3 us (2%)
    unnamed x2, blocking collectives  1110 us
    gather x18, local copies, waits for them, and re-layouts, arrange(): return jnp.take_along_axis(tensor, order[..., None], axis=2)  987 us
    unnamed x187, local copies, waits for them, and re-layouts  192 us
    gather x1, local copies, waits for them, and re-layouts, shards(): ok_key = jnp.take_along_axis(ok_heads, key_perm, axis=2).reshape(cshape)  97.2 us
    gather x1, local copies, waits for them, and re-layouts, shards(): seg_key = jnp.take_along_axis(seg_heads, key_perm, axis=2).reshape(cshape)  97.2 us
    gather x1, local copies, waits for them, and re-layouts, shards(): ok_query = jnp.take_along_axis(ok_heads, query_perm, axis=2).reshape(cshape)  97.2 us
    gather x1, local copies, waits for them, and re-layouts, shards(): jnp.take_along_axis(seg_heads, query_perm, axis=2).reshape(cshape)  97.2 us
    all_gather x1, waiting for transfers between devices, add_all(): pieces = lax.all_gather(array, mesh_axis)  79.8 us
  transfers between devices with their start and end apart: 5, of which 1 were waited for; matrix products, arithmetic and copies ran while one was open for 35% of the time, Pallas kernels for 0%

profile of v1, /device:TPU:0, one launch (start us, length us, event | category | flops | bytes accessed | tf_op | source)
XLA Modules:
  0.0 3157.3 jit_solution(6086148110228714409)
XLA Ops:
  13.8 97.2 %gather_fusion.2 = s32[12288]{0:T(1024)S(1)} fusion(s32[12,1024]{1,0:T(8,128)S(1)} %broadcast.664, s32[12288]{0:T(1024)S(1)} %bitcast.235), kind=kCustom, calls=%fused_computation.4.clone | custom fusion | bytes 196608 | tf_op jit(solution)/shard_map/jit(take_along_axis)/gather | solution.py:132
  111.1 97.2 %gather_fusion = s32[12288]{0:T(1024)S(1)} fusion(s32[12,1024]{1,0:T(8,128)S(1)} %broadcast.662, s32[12288]{0:T(1024)S(1)} %bitcast.236), kind=kCustom, calls=%fused_computation.clone | custom fusion | bytes 196608 | tf_op jit(solution)/shard_map/jit(take_along_axis)/gather | solution.py:130
  208.4 97.2 %gather_fusion.3 = s32[12288]{0:T(1024)S(1)} fusion(s32[12,1024]{1,0:T(8,128)S(1)} %broadcast.664, s32[12288]{0:T(1024)S(1)} %bitcast.237), kind=kCustom, calls=%fused_computation.5.clone | custom fusion | bytes 196608 | tf_op jit(solution)/shard_map/jit(take_along_axis)/gather | solution.py:133
  305.8 97.2 %gather_fusion.1 = s32[12288]{0:T(1024)S(1)} fusion(s32[12,1024]{1,0:T(8,128)S(1)} %broadcast.662, s32[12288]{0:T(1024)S(1)} %bitcast.238), kind=kCustom, calls=%fused_computation.3.clone | custom fusion | bytes 196608 | tf_op jit(solution)/shard_map/jit(take_along_axis)/gather | solution.py:131
  404.7 45.4 %scatter_custom_fusion.1 = s32[12288]{0:T(1024)S(1)} fusion(s32[12288]{0:T(1024)S(1)} %reshape.584, s32[12288]{0:T(1024)S(1)} %reshape.578, s32[]{:T(128)} %constant.17.clone.1), kind=kCustom, calls=%fused_computation.152 | custom fusion | bytes 49156
  450.9 45.4 %scatter_custom_fusion = s32[12288]{0:T(1024)S(1)} fusion(s32[12288]{0:T(1024)S(1)} %reshape.576, s32[12288]{0:T(1024)S(1)} %reshape.578, s32[]{:T(128)} %constant.17.clone.1), kind=kCustom, calls=%fused_computation.154 | custom fusion | bytes 49156
  499.6 38.8 %all-reduce.9 = (bf16[768]{0:T(1024)(128)(2,1)S(1)}, bf16[768]{0:T(1024)(128)(2,1)S(1)}, bf16[768]{0:T(1024)(128)(2,1)S(1)}, bf16[768]{0:T(1024)(128)(2,1)S(1)},...) all-reduce(bf16[768]{0:T(1024)(128)(2,1)S(1)} %dynamic-update-slice, ...), channel_id=1, replica_groups=mesh['rep'=4,'shard'=8] {'shard'}, use_global_device_ids=true, to_apply=%add | all-reduce | flops 6144 | bytes 24576
  540.2 25.9 all-gather.1
  572.3 5.8 fusion.28
  583.3 3.1 copy.97
  586.3 119.4 %gather_fusion.5 = bf16[12288,64]{1,0:T(8,128)(2,1)} fusion(bf16[12,1024,64]{2,1,0:T(8,128)(2,1)S(1)} %bitcast.239, s32[12288]{0:T(1024)S(1)} %bitcast.233), kind=kCustom, calls=%fused_computation.6.clone | custom fusion | bytes 3244032 | tf_op jit(solution)/shard_map/jit(take_along_axis)/gather | solution.py:55
  705.7 4.3 copy.98
  710.0 3.1 copy.102
  713.0 119.4 %gather_fusion.6 = bf16[12288,64]{1,0:T(8,128)(2,1)} fusion(bf16[12,1024,64]{2,1,0:T(8,128)(2,1)S(1)} %bitcast.240, s32[12288]{0:T(1024)S(1)} %bitcast.234), kind=kCustom, calls=%fused_computation.7.clone | custom fusion | bytes 3244032 | tf_op jit(solution)/shard_map/jit(take_along_axis)/gather | solution.py:55
  832.4 3.2 copy.103
  840.9 3.1 copy.94
  844.0 119.4 %gather_fusion.4 = bf16[12288,64]{1,0:T(8,128)(2,1)} fusion(bf16[12,1024,64]{2,1,0:T(8,128)(2,1)S(1)} %bitcast.241, s32[12288]{0:T(1024)S(1)} %bitcast.231), kind=kCustom, calls=%fused_computation.1.clone | custom fusion | bytes 3244032 | tf_op jit(solution)/shard_map/jit(take_along_axis)/gather | solution.py:55
  963.3 3.2 copy.95
  967.2 12.3 select_reduce_fusion
  979.6 4.9 fusion.12
  985.1 8.2 fusion.21
  993.4 119.5 %gather_fusion.7 = bf16[12288,64]{1,0:T(8,128)(2,1)} fusion(bf16[12,1024,64]{2,1,0:T(8,128)(2,1)S(1)} %bitcast.246, s32[12288]{0:T(1024)S(1)} %reshape.757), kind=kCustom, calls=%fused_computation.2.clone | custom fusion | bytes 3244032 | tf_op jit(solution)/shard_map/jit(take_along_axis)/gather | solution.py:55
  1112.9 3.1 copy.108
  1117.6 3.9 fusion.64
  1122.0 38.7 %multiply_convert_fusion = (bf16[1024,3072]{1,0:T(8,128)(2,1)}, f32[1024,3072]{1,0:T(8,128)}, f32[1024,3072]{1,0:T(8,128)}) fusion(f32[3072]{0:T(1024)S(1)} %bitcast.304, bf16[768,3072]{1,0:T(8,128)(2,1)} %all-gather.13.cloned.1.call-done, f32[1024,768]{0,1:T(8,128)S(1)} %get-tuple-element.122, f32[768]{0:T(1024)S(1)} %convert_element_type.136, ...), kind=kOutput, calls=%fused_computation.18 | convolution fusion | flops 5043388416 | bytes 39348224 | tf_op jit(solution)/shard_map/dot_general | solution.py:160
  1160.7 9.8 fusion.65
  1174.9 7.5 fusion.66
  1182.4 17.4 convert_reduce_fusion
  1199.9 10.6 fusion.57
  1210.5 9.0 multiply_reduce_fusion.1
  1226.3 3.1 copy.112
  1229.4 119.4 %gather_fusion.8 = bf16[12288,64]{1,0:T(8,128)(2,1)} fusion(bf16[12,1024,64]{2,1,0:T(8,128)(2,1)S(1)} %bitcast.242, s32[12288]{0:T(1024)S(1)} %bitcast.232), kind=kCustom, calls=%fused_computation.8.clone | custom fusion | bytes 3244032 | tf_op jit(solution)/shard_map/jit(take_along_axis)/gather | solution.py:55
  1348.8 3.2 copy.113
  1352.7 8.2 fusion.19
  1360.9 12.2 multiply_reduce_fusion
  1373.1 5.0 multiply_convert_fusion.1
  1378.2 3.4 convolution_multiply_fusion.1
  1384.1 9.0 reshape.436
  1393.2 3.5 reshape.432
  1396.7 120.2 %gather_fusion.11 = bf16[12288,64]{1,0:T(8,128)(2,1)} fusion(bf16[12,1024,64]{2,1,0:T(8,128)(2,1)S(1)} %bitcast.245, s32[12288]{0:T(1024)S(1)} %copy-done.4), kind=kCustom, calls=%fused_computation.11.clone | custom fusion | bytes 3244032 | tf_op jit(solution)/shard_map/jit(take_along_axis)/gather | solution.py:55
  1516.9 4.5 copy.130
  1521.4 9.0 reshape.438
  1530.3 3.1 copy.143
  1533.4 120.3 %gather_fusion.9 = bf16[12288,64]{1,0:T(8,128)(2,1)} fusion(bf16[12,1024,64]{2,1,0:T(8,128)(2,1)S(1)} %bitcast.243, s32[12288]{0:T(1024)S(1)} %copy-done.6), kind=kCustom, calls=%fused_computation.9.clone | custom fusion | bytes 3244032 | tf_op jit(solution)/shard_map/jit(take_along_axis)/gather | solution.py:55
  1653.7 3.1 copy.120
  1658.9 3.1 copy.144
  1662.0 120.3 %gather_fusion.10 = bf16[12288,64]{1,0:T(8,128)(2,1)} fusion(bf16[12,1024,64]{2,1,0:T(8,128)(2,1)S(1)} %bitcast.244, s32[12288]{0:T(1024)S(1)} %copy-done.4), kind=kCustom, calls=%fused_computation.10.clone | custom fusion | bytes 3244032 | tf_op jit(solution)/shard_map/jit(take_along_axis)/gather | solution.py:55
  1782.3 4.3 copy.125
  1786.6 4.2 select_convert_fusion.1
  1791.2 8.9 convolution_bitcast_fusion
  1800.1 8.0 copy.132
  1808.1 7.2 reshape.429
  1815.3 5.3 constant_dynamic-update-slice_fusion
  1823.7 7.5 dynamic-update-slice.11
  1835.4 26.4 dynamic-update-slice.15
  1863.2 26.0 dynamic-update-slice.17
  1893.5 1069.1 %all-reduce.11 = bf16[8,885888]{1,0:T(8,128)(2,1)} all-reduce(f32[8,885888]{1,0:T(8,128)} %dynamic-update-slice.20), channel_id=3, replica_groups=mesh['rep'=4,'shard'=8] {'shard'}, use_global_device_ids=true, to_apply=%region_22.26.clone | all-reduce | flops 7087104 | bytes 42522624
  2962.6 8.9 fusion.11
  2973.1 7.8 fusion.30
  2982.5 79.8 %all-gather.17.cloned.1.call-done = bf16[4,1,885888]{2,1,0:T(2,128)(2,1)} async-done(((bf16[1,1,885888]{2,1,0:T(2,128)(2,1)}), bf16[4,1,885888]{2,1,0:T(2,128)(2,1)}) %all-gather.17.cloned.1.call-update) | async-done | bytes 7087120 | tf_op jit(solution)/shard_map/all_gather | solution.py:12
  3062.2 38.3 %reduce.17 = bf16[885888]{0:T(1024)(128)(2,1)S(1)} reduce(bf16[4,1,885888]{2,1,0:T(2,128)(2,1)} %all-gather.17.cloned.1.call-done, bf16[]{:T(256)} %constant.59.clone.1), dimensions={0,1}, to_apply=%region_23.27 | reduce | flops 2657664 | bytes 8858882 | tf_op jit(solution)/shard_map/reduce_sum | solution.py:13
  3100.6 20.2 reshape.473
  3123.5 9.3 slice_reduce_fusion.2
  3132.8 12.5 slice_reduce_fusion
  (277 shorter events, 73.7 us)
Async XLA Ops:
  7.2 6.6 copy-start
  7.2 565.1 %all-gather.9.cloned.1.call-start = ((), (), s32[]{:S(2)}) async-start(), calls=%async_computation | async-start | bytes 3981312 | tf_op jit(solution)/shard_map/all_gather | solution.py:90
  7.9 1109.7 %all-gather.11.cloned.1.call-start = ((), (), s32[]{:S(2)}) async-start(), calls=%async_computation.1 | async-start | bytes 1327104 | tf_op jit(solution)/shard_map/all_gather | solution.py:93
  8.7 1113.3 %all-gather.13.cloned.1.call-start = ((), (), s32[]{:S(2)}) async-start(), calls=%async_computation.2 | async-start | bytes 5308416 | tf_op jit(solution)/shard_map/all_gather | solution.py:97
  9.4 1151.3 %all-gather.15.cloned.1.call-start = ((), (), s32[]{:S(2)}) async-start(), calls=%async_computation.3 | async-start | bytes 5308416 | tf_op jit(solution)/shard_map/all_gather | solution.py:99
  10.0 3052.2 %all-gather.17.cloned.1.call-start = ((), (), s32[]{:S(2)}) async-start(), calls=%async_computation.4 | async-start | bytes 17717760 | tf_op jit(solution)/shard_map/all_gather | solution.py:12
  11.9 832.0 %copy-start.2 = (s32[12,1024,1]{1,2,0:T(1,128)}, s32[12,1024,1]{1,2,0:T(1,128)S(1)}, u32[]{:S(2)}) copy-start(s32[12,1024,1]{1,2,0:T(1,128)S(1)} %get-tuple-element.110) | copy-start | bytes 147460
  13.8 97.3 %copy-start.49 = (s32[1,1024]{1,0:T(1,128)S(1)}, s32[1,1024]{1,0:T(1,128)}, u32[]{:S(2)}) copy-start(s32[1,1024]{1,0:T(1,128)} %param.39) | copy-start | bytes 12292
  305.6 97.5 %copy-start.30 = (s32[1,12,1024]{2,0,1:T(1,128)S(1)}, s32[1,12,1024]{2,0,1:T(1,128)}, u32[]{:S(2)}) copy-start(s32[1,12,1024]{2,0,1:T(1,128)} %param.41) | copy-start | bytes 147460
  305.6 97.6 %copy-start.31 = (s32[1,12,1024]{2,0,1:T(1,128)S(1)}, s32[1,12,1024]{2,0,1:T(1,128)}, u32[]{:S(2)}) copy-start(s32[1,12,1024]{2,0,1:T(1,128)} %param.42) | copy-start | bytes 147460
  305.6 97.8 %copy-start.54 = (s32[3]{0:T(128)S(1)}, s32[3]{0:T(128)}, u32[]{:S(2)}) copy-start(s32[3]{0:T(128)} %constant.127) | copy-start | bytes 40
  305.6 98.4 %copy-start.53 = (s32[3]{0:T(128)S(1)}, s32[3]{0:T(128)}, u32[]{:S(2)}) copy-start(s32[3]{0:T(128)} %constant.130) | copy-start | bytes 40
  305.6 190.7 %copy-start.52 = (bf16[384]{0:T(512)(128)(2,1)S(1)}, bf16[384]{0:T(512)(128)(2,1)}, u32[]{:S(2)}) copy-start(bf16[384]{0:T(512)(128)(2,1)} %param.34) | copy-start | bytes 2308
  305.7 190.8 %copy-start.51 = (u32[32]{0:T(128)S(1)}, u32[32]{0:T(128)}, u32[]{:S(2)}) copy-start(u32[32]{0:T(128)} %constant.302) | copy-start | bytes 388
  305.7 192.0 %copy-start.56 = (bf16[96]{0:T(256)(128)(2,1)S(1)}, bf16[96]{0:T(256)(128)(2,1)}, u32[]{:S(2)}) copy-start(bf16[96]{0:T(256)(128)(2,1)} %param.37) | copy-start | bytes 580
  305.7 192.2 %copy-start.57 = (bf16[96]{0:T(256)(128)(2,1)S(1)}, bf16[96]{0:T(256)(128)(2,1)}, u32[]{:S(2)}) copy-start(bf16[96]{0:T(256)(128)(2,1)} %param.36) | copy-start | bytes 580
  305.7 192.5 %copy-start.58 = (bf16[96]{0:T(256)(128)(2,1)S(1)}, bf16[96]{0:T(256)(128)(2,1)}, u32[]{:S(2)}) copy-start(bf16[96]{0:T(256)(128)(2,1)} %param.31) | copy-start | bytes 580
  305.7 192.7 %copy-start.59 = (bf16[96]{0:T(256)(128)(2,1)S(1)}, bf16[96]{0:T(256)(128)(2,1)}, u32[]{:S(2)}) copy-start(bf16[96]{0:T(256)(128)(2,1)} %param.32) | copy-start | bytes 580
  305.7 192.9 %copy-start.60 = (bf16[96]{0:T(256)(128)(2,1)S(1)}, bf16[96]{0:T(256)(128)(2,1)}, u32[]{:S(2)}) copy-start(bf16[96]{0:T(256)(128)(2,1)} %param.30) | copy-start | bytes 580
  305.7 193.1 %copy-start.61 = (bf16[96]{0:T(256)(128)(2,1)S(1)}, bf16[96]{0:T(256)(128)(2,1)}, u32[]{:S(2)}) copy-start(bf16[96]{0:T(256)(128)(2,1)} %param.28) | copy-start | bytes 580
  305.7 193.4 %copy-start.62 = (bf16[96]{0:T(256)(128)(2,1)S(1)}, bf16[96]{0:T(256)(128)(2,1)}, u32[]{:S(2)}) copy-start(bf16[96]{0:T(256)(128)(2,1)} %param.27) | copy-start | bytes 580
  305.8 193.6 %copy-start.63 = (bf16[96]{0:T(256)(128)(2,1)S(1)}, bf16[96]{0:T(256)(128)(2,1)}, u32[]{:S(2)}) copy-start(bf16[96]{0:T(256)(128)(2,1)} %param.38) | copy-start | bytes 580
  403.0 164.4 %copy-start.25 = (bf16[1,1024,768]{2,1,0:T(8,128)(2,1)S(1)}, bf16[1,1024,768]{2,1,0:T(8,128)(2,1)}, u32[]{:S(2)}) copy-start(bf16[1,1024,768]{2,1,0:T(8,128)(2,1)} %param.43) | copy-start | bytes 4718596
  403.2 581.9 %copy-start.32 = (s32[1,12,1024]{2,0,1:T(1,128)}, s32[1,12,1024]{2,0,1:T(1,128)S(1)}, u32[]{:S(2)}) copy-start(s32[1,12,1024]{2,0,1:T(1,128)S(1)} %get-tuple-element.108) | copy-start | bytes 147460
  403.4 581.7 %copy-start.34 = (s32[1,12,1024]{2,0,1:T(1,128)}, s32[1,12,1024]{2,0,1:T(1,128)S(1)}, u32[]{:S(2)}) copy-start(s32[1,12,1024]{2,0,1:T(1,128)S(1)} %get-tuple-element.106) | copy-start | bytes 147460
  496.3 619.7 %copy-start.37 = (pred[12,1024]{1,0:T(8,128)(4,1)}, pred[12,1024]{1,0:T(8,128)(4,1)S(1)}, u32[]{:S(2)}) copy-start(pred[12,1024]{1,0:T(8,128)(4,1)S(1)} %and_bitcast_fusion.1) | copy-start | bytes 36868
  566.1 400.4 %copy-start.39 = (pred[1,12,1024,1]{2,1,3,0:T(8,128)(4,1)}, pred[1,12,1024,1]{2,1,3,0:T(8,128)(4,1)S(1)}, u32[]{:S(2)}) copy-start(pred[1,12,1024,1]{2,1,3,0:T(8,128)(4,1)S(1)} %copy.184) | copy-start | bytes 36868
  566.4 418.6 %copy-start.41 = (pred[12,8,128]{2,1,0:T(8,128)(4,1)}, pred[12,8,128]{2,1,0:T(8,128)(4,1)S(1)}, u32[]{:S(2)}) copy-start(pred[12,8,128]{2,1,0:T(8,128)(4,1)S(1)} %slice.147) | copy-start | bytes 36868
  566.7 418.4 %copy-start.43 = (pred[12,8,128]{2,1,0:T(8,128)(4,1)}, pred[12,8,128]{2,1,0:T(8,128)(4,1)S(1)}, u32[]{:S(2)}) copy-start(pred[12,8,128]{2,1,0:T(8,128)(4,1)S(1)} %slice.148) | copy-start | bytes 36868
  567.4 426.0 %copy-start.5 = (s32[12288]{0:T(1024)}, s32[12288]{0:T(1024)S(1)}, u32[]{:S(2)}) copy-start(s32[12288]{0:T(1024)S(1)} %reshape.757) | copy-start | bytes 147460
  568.6 9.5 copy-start.8
  568.6 3.6 copy-start.26
  832.4 3.2 copy-start.22
  836.0 3.3 copy-start.23
  963.3 3.9 copy-start.17
  967.2 12.3 copy-start.19
  979.5 13.8 copy-start.7
  979.6 5.5 copy-start.27
  1121.5 39.2 %copy-start.10 = (f32[1024,768]{0,1:T(8,128)}, f32[1024,768]{0,1:T(8,128)S(1)}, u32[]{:S(2)}) copy-start(f32[1024,768]{0,1:T(8,128)S(1)} %get-tuple-element.122) | copy-start | bytes 9437188
  1122.0 38.7 %copy-start.50 = (f32[768]{0:T(1024)S(1)}, f32[768]{0:T(1024)}, u32[]{:S(2)}) copy-start(f32[768]{0:T(1024)} %convert_element_type.140) | copy-start | bytes 9220
  1160.7 10.2 copy-start.9
  1160.7 10.2 copy-start.46
  1170.9 4.0 slice-start.2
  1199.9 10.6 copy-start.11
  1199.9 10.6 copy-start.64
  1348.8 3.2 copy-start.40
  1348.8 3.9 copy-start.33
  1348.8 3.9 copy-start.35
  1348.8 3.9 copy-start.36
  1348.8 3.9 copy-start.42
  1348.8 3.9 copy-start.44
  1352.0 8.9 slice-start
  1352.7 8.2 slice-start.1
  1352.7 8.2 copy-start.28
  1373.1 5.1 copy-start.20
  1378.2 3.4 copy-start.18
  1393.1 3.6 copy-start.4
  1782.3 4.3 copy-start.45
  1786.6 4.6 copy-start.14
  1790.8 9.3 copy-start.21
  1815.3 8.4 copy-start.12
  1863.2 28.9 copy-start.48
  2962.6 9.0 copy-start.16
  3132.8 17.8 copy-start.1
  (10 other events, 23.9 us)
Sparse Core Ops, SparseCore 0:
  10.2 67.8 all-gather.8
  80.3 39.5 all-gather.10
  122.1 78.6 all-gather.12
  202.8 78.0 all-gather.14
  2971.7 90.5 all-gather.16
